TPU v7x, 32 devices: a whole 2x2x4 slice. The times are simulated.
32 devices in a mesh: grp: 4 (over y, x), tile: 8 (over z, core).
Axes of the slice: x: 2, y: 2, z: 4, core: 2. Of those that a mesh axis runs over, the one named last changes fastest.
Arguments:
- temp: bfloat16 [48, 64, 2048], P(None, 'grp', 'tile'), may hold values from -6 to 6
- humid: bfloat16 [48, 64, 2048], P(None, 'grp', 'tile'), may hold values from -5 to 5
- parent: int32 [64, 2048], P('grp', 'tile'), may hold values from 0 to 8191, as said below
- kabs: float32 [112, 48], replicated, may hold values from 0.003 to 1
- planck: float32 [112], replicated, may hold values from 0.5 to 2
- top_flux: float32 [112], replicated, may hold values from 0 to 2
Outputs:
- temp_next: bfloat16 [48, 64, 2048], P(None, 'grp', 'tile')
Inputs may be any that keep to these rules, and one draw needn't show every extreme that they name: parent // 1024 is the tile index, in the same region, of the device owning that parent column; the fine cells of one device name any one owner at most 1024 times.
All inputs are finite; a program needn't handle non-finite values.
Results may differ from a plain program's by a relative error of at most 0.005.
Values may be sent and summed in bfloat16 or wider, within the bound.
A program may use at most 64 MiB of HBM per device.

v0:
```python
import functools
import math

import jax
import jax.numpy as jnp
from jax import lax
from jax.experimental import pallas as pl
from jax.experimental.pallas import tpu as pltpu
from jax.sharding import PartitionSpec as P

F32 = jnp.float32
BF16 = jnp.bfloat16
VMEM_LIMIT = 60 * 1024 * 1024
VSPEC = pl.BlockSpec(memory_space=pltpu.VMEM)


def partial_kernel(chunks, offset_ref, temp_ref, humid_ref, parent_ref, out_ref, onehot, masked):
    rows, levels, lanes = temp_ref.shape
    step = pl.program_id(0)
    owner = 2 * step + offset_ref[0]
    data = 2 * levels * chunks
    row = lax.broadcasted_iota(jnp.int32, (16, lanes), 0)

    @pl.when(step == 0)
    def _():
        lo_iota = lax.broadcasted_iota(jnp.int32, (lanes, lanes), 0)
        for r in range(rows):
            low = parent_ref[r : r + 1, :] % lanes
            onehot[:, r * lanes : (r + 1) * lanes] = (lo_iota == low).astype(F32).astype(BF16)

    for r in range(rows):
        high = jnp.broadcast_to(parent_ref[r : r + 1, :] // lanes, (16, lanes))
        part = slice(r * lanes, (r + 1) * lanes)
        for c in range(chunks):
            mask = (high == owner * chunks + c).astype(F32).astype(BF16)
            for v in range(levels // 16):
                src = slice(v * 16, (v + 1) * 16)
                at = c * 2 * levels + v * 16
                masked[at : at + 16, part] = temp_ref[r, src, :] * mask
                masked[at + levels : at + levels + 16, part] = humid_ref[r, src, :] * mask
        masked[data : data + 16, part] = (high == owner * chunks + row // 2).astype(F32).astype(BF16)
    total = lax.dot_general(
        masked[...], onehot[...], (((1,), (1,)), ((), ())), preferred_element_type=F32
    )
    out_ref[0, :data, :] = total[:data].astype(out_ref.dtype)
    count = total[data:]
    high = jnp.floor(count * (1.0 / 32.0))
    out_ref[0, data:, :] = jnp.where(row % 2 == 0, high, count - 32.0 * high).astype(out_ref.dtype)


def radiate_kernel(levels, feats, recv_ref, kabs_in, planck_ref, top_ref, out_ref, kabs_ref, sums, absorb, emit, trans, net, heat):
    tiles = recv_ref.shape[0]
    lanes = recv_ref.shape[2]
    chunks = recv_ref.shape[1] // feats
    octets = kabs_in.shape[0] // 8
    group = octets // 2 if octets % 2 == 0 else octets
    width = 128
    data = chunks * feats
    for k in range(levels):
        kabs_ref[k] = jnp.broadcast_to(kabs_in[:, k : k + 1], kabs_ref.shape[1:])

    def add(i, carry):
        at = pl.ds(pl.multiple_of(i * 16, 16), 16)
        acc = recv_ref[0, at, :].astype(F32)
        for s in range(1, tiles):
            acc = acc + recv_ref[s, at, :].astype(F32)
        sums[at, :] = acc
        return carry

    lax.fori_loop(0, data // 16 + 1, add, 0)
    for c in range(chunks):
        base = c * feats
        cnt = sums[data + 2 * c : data + 2 * c + 1, :] * 32.0
        cnt = cnt + sums[data + 2 * c + 1 : data + 2 * c + 2, :]
        cnt = jnp.maximum(cnt, 1.0)
        for j in range(lanes // width):
            part = slice(j * width, (j + 1) * width)
            ct = c * (lanes // width) + j
            tc = sums[base : base + levels, part] / cnt[:, part]
            hc = sums[base + levels : base + 2 * levels, part] / cnt[:, part]
            emit[ct] = jnp.exp(0.25 * tc)
            absorb[ct] = jnp.exp(0.5 * hc) * (-math.log2(math.e))
            heat[ct] = -0.5 * hc

    scale = levels / (octets * 8)

    def column(ct, carry):
        for half in range(octets // group):
            gs = [(half * group + p) * 8 for p in range(group)]
            planck = [jnp.broadcast_to(planck_ref[g : g + 8, :], (8, width)) for g in gs]
            down = [jnp.broadcast_to(top_ref[g : g + 8, :], (8, width)) for g in gs]
            if half == 0:
                before = sum(down[1:], down[0])
                net[0] = before
            else:
                net[0] = net[0] + sum(down[1:], down[0])
            for k in range(levels):
                ab = absorb[ct, k : k + 1, :]
                em = emit[ct, k : k + 1, :]
                acc = None
                for p in range(group):
                    t = jnp.exp2(kabs_ref[k, gs[p] : gs[p] + 8, :] * ab)
                    trans[k, p] = t
                    s = planck[p] * em
                    down[p] = s + t * (down[p] - s)
                    acc = down[p] if acc is None else acc + down[p]
                net[k + 1] = acc if half == 0 else net[k + 1] + acc
            up = [0.3 * d for d in down]
            for k in range(levels - 1, -1, -1):
                em = emit[ct, k : k + 1, :]
                acc = None
                for p in range(group):
                    s = planck[p] * em
                    up[p] = s + trans[k, p] * (up[p] - s)
                    acc = up[p] if acc is None else acc + up[p]
                net[k + 1] = net[k + 1] - acc
            net[0] = net[0] - acc
        for k in range(levels):
            row = jnp.sum(net[k] - net[k + 1], axis=0, keepdims=True) * scale
            heat[ct, k : k + 1, :] = heat[ct, k : k + 1, :] + row
        return carry

    lax.fori_loop(0, chunks * lanes // width, column, 0)
    per = lanes // width
    for c in range(chunks):
        for j in range(per):
            out_ref[c * levels : (c + 1) * levels, j * width : (j + 1) * width] = heat[c * per + j].astype(BF16)


def laplace_row(centre, above, below, left, right):
    lanes = centre.shape[1]
    lane = lax.broadcasted_iota(jnp.int32, centre.shape, 1)
    west = jnp.where(lane == 0, left, pltpu.roll(centre, 1, 1))
    east = jnp.where(lane == lanes - 1, right, pltpu.roll(centre, lanes - 1, 1))
    return above + below + west + east - 4.0 * centre


def gather_kernel(levels, table_ref, parent_ref, temp_ref, humid_ref, up_ref, dn_ref, lf_ref, rt_ref, out_ref):
    rows, _, lanes = temp_ref.shape
    tiles = table_ref.shape[0]
    chunks = table_ref.shape[1] // levels
    lo_iota = lax.broadcasted_iota(jnp.int32, (lanes, lanes), 0)
    for r in range(rows):
        low = parent_ref[r : r + 1, :] % lanes
        high = jnp.broadcast_to(parent_ref[r : r + 1, :] // lanes, (levels, lanes))
        onehot = (lo_iota == low).astype(F32).astype(BF16)

        def owner(i, acc):
            span = 4
            got = jnp.dot(
                table_ref[pl.ds(i * span, span)].reshape(span * chunks * levels, lanes),
                onehot,
                preferred_element_type=F32,
            )
            for c in range(span * chunks):
                acc = jnp.where(high == i * span * chunks + c, got[c * levels : (c + 1) * levels], acc)
            return acc

        picked = lax.fori_loop(0, tiles // 4, owner, jnp.zeros((levels, lanes), F32))
        centre = temp_ref[r].astype(F32)
        above = (temp_ref[r - 1] if r > 0 else up_ref[0]).astype(F32)
        below = (temp_ref[r + 1] if r < rows - 1 else dn_ref[0]).astype(F32)
        lap = laplace_row(centre, above, below, lf_ref[:, r : r + 1], rt_ref[:, r : r + 1])
        first = (centre + 0.2 * lap).astype(BF16).astype(F32)
        heat_f = picked + 0.5 * humid_ref[r].astype(F32)
        out_ref[r] = (first + 0.5 * heat_f).astype(BF16)


def laplace_kernel(x_ref, up_ref, dn_ref, lf_ref, rt_ref, out_ref):
    rows = x_ref.shape[0]
    for r in range(rows):
        centre = x_ref[r].astype(F32)
        above = (x_ref[r - 1] if r > 0 else up_ref[0]).astype(F32)
        below = (x_ref[r + 1] if r < rows - 1 else dn_ref[0]).astype(F32)
        lap = laplace_row(centre, above, below, lf_ref[:, r : r + 1], rt_ref[:, r : r + 1])
        out_ref[r] = (centre + 0.2 * lap).astype(BF16)


def halos(x):
    g, t = lax.axis_size("grp"), lax.axis_size("tile")
    ahead = lambda n: [(i, (i + 1) % n) for i in range(n)]
    back = lambda n: [((i + 1) % n, i) for i in range(n)]
    up = lax.ppermute(x[-1:], "grp", ahead(g))
    dn = lax.ppermute(x[:1], "grp", back(g))
    lf = lax.ppermute(jnp.transpose(x[:, :, -1]), "tile", ahead(t)).astype(F32)
    rt = lax.ppermute(jnp.transpose(x[:, :, 0]), "tile", back(t)).astype(F32)
    return up, dn, lf, rt


def on_device(temp, humid, parent, kabs, planck, top_flux):
    levels, rows, lanes = temp.shape
    tiles = lax.axis_size("tile")
    owned = rows * lanes // 4
    chunks = owned // lanes
    feats = 2 * levels
    gpts = kabs.shape[0]
    params = pltpu.CompilerParams(vmem_limit_bytes=VMEM_LIMIT)

    x = jnp.transpose(temp, (1, 0, 2))
    h = jnp.transpose(humid, (1, 0, 2))
    size = chunks * feats + 16
    core = lax.rem(lax.axis_index("tile"), 2)
    half = tiles // 2

    def partial_sums(offset, dtype):
        return pl.pallas_call(
            functools.partial(partial_kernel, chunks),
            out_shape=jax.ShapeDtypeStruct((half, size, lanes), dtype),
            grid=(half,),
            in_specs=[
                pl.BlockSpec(memory_space=pltpu.SMEM),
                pl.BlockSpec((rows, levels, lanes), lambda i: (0, 0, 0)),
                pl.BlockSpec((rows, levels, lanes), lambda i: (0, 0, 0)),
                pl.BlockSpec((rows, lanes), lambda i: (0, 0)),
            ],
            out_specs=pl.BlockSpec((1, size, lanes), lambda i: (i, 0, 0)),
            scratch_shapes=[
                pltpu.VMEM((lanes, rows * lanes), BF16),
                pltpu.VMEM((size, rows * lanes), BF16),
            ],
            compiler_params=params,
            cost_estimate=pl.CostEstimate(
                flops=2 * half * size * rows * lanes * lanes,
                bytes_accessed=4 * half * size * lanes,
                transcendentals=0,
            ),
        )(offset.reshape(1).astype(jnp.int32), x, h, parent)

    theirs = partial_sums(1 - core, BF16)
    given = lax.ppermute(theirs, "tile", [(i, i ^ 1) for i in range(tiles)])
    mine = partial_sums(core, F32)
    partial = (mine + given.astype(F32)).astype(BF16)
    groups = [list(range(c, tiles, 2)) for c in range(2)]
    recv = lax.all_to_all(
        partial, "tile", split_axis=0, concat_axis=0, tiled=True, axis_index_groups=groups
    )

    ctiles = owned // 128
    octets = gpts // 8
    group = octets // 2 if octets % 2 == 0 else octets
    table = pl.pallas_call(
        functools.partial(radiate_kernel, levels, feats),
        out_shape=jax.ShapeDtypeStruct((chunks * levels, lanes), BF16),
        in_specs=[VSPEC] * 4,
        out_specs=VSPEC,
        scratch_shapes=[
            pltpu.VMEM((levels, gpts, 128), F32),
            pltpu.VMEM((size, lanes), F32),
            pltpu.VMEM((ctiles, levels, 128), F32),
            pltpu.VMEM((ctiles, levels, 128), F32),
            pltpu.VMEM((levels, group, 8, 128), F32),
            pltpu.VMEM((levels + 1, 8, 128), F32),
            pltpu.VMEM((ctiles, levels, 128), F32),
        ],
        compiler_params=params,
    )(recv, kabs, planck[:, None], top_flux[:, None])
    tables = lax.all_gather(table, "tile", axis=0)

    second = pl.pallas_call(
        functools.partial(gather_kernel, levels),
        out_shape=jax.ShapeDtypeStruct((rows, levels, lanes), BF16),
        in_specs=[VSPEC] * 8,
        out_specs=VSPEC,
        compiler_params=params,
    )(tables, parent, x, h, *halos(x))
    out = pl.pallas_call(
        laplace_kernel,
        out_shape=jax.ShapeDtypeStruct((rows, levels, lanes), BF16),
        in_specs=[VSPEC] * 5,
        out_specs=VSPEC,
        compiler_params=params,
    )(second, *halos(second))
    return jnp.transpose(out, (1, 0, 2))


def solution(mesh):
    return jax.shard_map(
        on_device,
        mesh=mesh,
        in_specs=(P(None, "grp", "tile"), P(None, "grp", "tile"), P("grp", "tile"), P(), P(), P()),
        out_specs=P(None, "grp", "tile"),
        check_vma=False,
    )
```

profile of v0, /device:TPU:0, one launch (start us, length us, event | category | flops | bytes accessed | tf_op | source)
XLA Modules:
  0.0 109.5 jit_solution(12303522389427395330)
XLA Ops:
  0.0 1.9 %copy.37 = bf16[48,16,256]{2,0,1:T(8,128)(2,1)} copy(bf16[48,16,256]{2,1,0:T(8,128)(2,1)} %param.7) | data formatting | bytes 786432 | tf_op args[1]
  1.9 1.9 %copy.22.temp_ref = bf16[16,48,256]{2,1,0:T(8,128)(2,1)} copy(bf16[16,48,256]{2,0,1:T(8,128)(2,1)} %bitcast.28) | data formatting | bytes 786432 | tf_op jit(solution)/shard_map/transpose | solution.py:199
  3.7 6.4 %shard_map.65 = bf16[4,400,256]{2,1,0:T(8,128)(2,1)} custom-call(s32[1]{0:T(128)} %bitcast.4.offset_ref, bf16[16,48,256]{2,1,0:T(8,128)(2,1)} %copy.22.temp_ref, bf16[16,48,256]{2,1,0:T(8,128)(2,1)} %bitcast.30, s32[16,256]{1,0:T(8,128)} %parent_ref.5), custom_call_target="tpu_custom_call" | custom-call | flops 3355443200 | bytes 1638400 | tf_op jit(solution)/shard_map/pallas_call | solution.py:206
  10.7 6.5 %shard_map.64 = f32[4,400,256]{2,1,0:T(8,128)} custom-call(s32[1]{0:T(128)} %bitcast.offset_ref, bf16[16,48,256]{2,1,0:T(8,128)(2,1)} %copy.22.temp_ref, bf16[16,48,256]{2,1,0:T(8,128)(2,1)} %bitcast.31, s32[16,256]{1,0:T(8,128)} %parent_ref.5), custom_call_target="tpu_custom_call" | custom-call | flops 3355443200 | bytes 1638400 | tf_op jit(solution)/shard_map/pallas_call | solution.py:206
  17.2 2.6 %add_convert_fusion = bf16[4,400,256]{2,1,0:T(8,128)(2,1)} fusion(f32[4,400,256]{2,1,0:T(8,128)} %shard_map.64, bf16[4,400,256]{2,1,0:T(8,128)(2,1)S(1)} %collective-permute-done), kind=kLoop, calls=%fused_computation | loop fusion | flops 1228800 | bytes 3276800 | tf_op jit(solution)/shard_map/convert_element_type | solution.py:232
  19.8 5.9 %all-to-all-start = ((bf16[4,400,256]{2,1,0:T(8,128)(2,1)}), bf16[4,400,256]{2,1,0:T(8,128)(2,1)}, u32[]{:S(2)}, u32[]{:S(2)}) async-start(bf16[4,400,256]{2,1,0:T(8,128)(2,1)} %add_convert_fusion), calls=%async_computation | async-start | bytes 1638400 | tf_op jit(solution)/shard_map/all_to_all | solution.py:234
  25.6 2.9 %copy.20 = bf16[48,16,256]{1,0,2:T(8,128)(2,1)S(1)} copy(bf16[48,16,256]{2,1,0:T(8,128)(2,1)S(1)} %copy-done.1) | data formatting | bytes 786432 | tf_op args[0]
  28.9 3.3 %collective-permute-start.4 = (bf16[48,16]{1,0:T(8,128)(2,1)S(1)}, bf16[48,16]{1,0:T(8,128)(2,1)S(1)}, u32[]{:S(2)}, u32[]{:S(2)}) collective-permute-start(bf16[48,16]{1,0:T(8,128)(2,1)S(1)} %get-tuple-element.5), channel_id=1, source_target_pairs={{1,0},{2,1},{3,2},{4,3},{5,4},{6,5},{7,6},{0,7},{9,8},{10,9},{11,1... | collective-permute-start | bytes 4616 | tf_op jit(solution)/shard_map/ppermute | solution.py:186
  32.2 4.0 %fusion = (bf16[1,48,256]{0,1,2:T(8,128)(2,1)}, bf16[1,48,256]{0,1,2:T(8,128)(2,1)}) fusion(bf16[16,48,256]{0,1,2:T(8,128)(2,1)S(1)} %bitcast.26), kind=kLoop, calls=%fused_computation.4 | loop fusion | bytes 98304 | tf_op jit(solution)/shard_map/slice | solution.py:184
  36.2 4.7 %copy.27 = bf16[1,48,256]{2,1,0:T(8,128)(2,1)S(1)} copy(bf16[1,48,256]{0,1,2:T(8,128)(2,1)} %get-tuple-element.8) | data formatting | bytes 49152 | tf_op jit(solution)/shard_map/slice | solution.py:183
  40.9 1.5 %collective-permute-start.1 = (bf16[1,48,256]{2,1,0:T(8,128)(2,1)S(1)}, bf16[1,48,256]{2,1,0:T(8,128)(2,1)S(1)}, u32[]{:S(2)}, u32[]{:S(2)}) collective-permute-start(bf16[1,48,256]{2,1,0:T(8,128)(2,1)S(1)} %copy.27), channel_id=1, source_target_pairs={{0,8},{8,16},{16,24},{24,0},{1,9},{9,17},{17,25},{25,1},{2,10},{10... | collective-permute-start | bytes 73736 | tf_op jit(solution)/shard_map/ppermute | solution.py:183
  42.5 2.6 %copy.28 = bf16[1,48,256]{2,1,0:T(8,128)(2,1)S(1)} copy(bf16[1,48,256]{0,1,2:T(8,128)(2,1)S(1)} %copy-done) | data formatting | bytes 49152 | tf_op jit(solution)/shard_map/slice | solution.py:184
  45.0 1.5 %collective-permute-start.2 = (bf16[1,48,256]{2,1,0:T(8,128)(2,1)S(1)}, bf16[1,48,256]{2,1,0:T(8,128)(2,1)S(1)}, u32[]{:S(2)}, u32[]{:S(2)}) collective-permute-start(bf16[1,48,256]{2,1,0:T(8,128)(2,1)S(1)} %copy.28), channel_id=1, source_target_pairs={{8,0},{16,8},{24,16},{0,24},{9,1},{17,9},{25,17},{1,25},{10,2},{18... | collective-permute-start | bytes 73736 | tf_op jit(solution)/shard_map/ppermute | solution.py:184
  47.9 0.7 copy.26.top_ref
  49.9 12.5 %shard_map.66 = bf16[192,256]{1,0:T(8,128)(2,1)} custom-call(bf16[4,400,256]{2,1,0:T(8,128)(2,1)} %all-to-all-done.recv_ref, f32[112,48]{1,0:T(8,128)} %copy.24.kabs_in, f32[112,1]{1,0:T(8,128)} %copy.25.planck_ref, f32[112,1]{1,0:T(8,128)} %copy.26.top_ref), custom_call_target="tpu_custom_call" | custom-call | tf_op jit(solution)/shard_map/pallas_call | solution.py:241
  62.4 16.8 %all-gather = bf16[1536,256]{1,0:T(8,128)(2,1)} all-gather(bf16[192,256]{1,0:T(8,128)(2,1)} %shard_map.66), channel_id=2, replica_groups=mesh['grp'=4,'tile'=8] {'tile'}, dimensions={0}, use_global_device_ids=true | all-gather | bytes 884736 | tf_op jit(solution)/shard_map/all_gather | solution.py:257
  79.9 12.8 %shard_map.67.x_ref = bf16[16,48,256]{2,1,0:T(8,128)(2,1)} custom-call(bf16[8,192,256]{2,1,0:T(8,128)(2,1)} %bitcast.27, s32[16,256]{1,0:T(8,128)} %parent_ref.5, bf16[16,48,256]{2,1,0:T(8,128)(2,1)} %copy.22.temp_ref, bf16[16,48,256]{2,1,0:T(8,128)(2,1)} %bitcast.32, bf16[1,48,256]{2,1,0:T(8,128)(2,1)} %copy-done.2, bf16[1,48,256]{2,1,0:T(8,128)(2,1)} %copy-done.4, ...), custom_call_target="tpu_custom_call" | custom-call | tf_op jit(solution)/shard_map/pallas_call | solution.py:259
  92.7 0.8 fusion.2
  94.0 2.4 %collective-permute-start.6 = (bf16[1,48,256]{2,1,0:T(8,128)(2,1)S(1)}, bf16[1,48,256]{2,1,0:T(8,128)(2,1)S(1)}, u32[]{:S(2)}, u32[]{:S(2)}) collective-permute-start(bf16[1,48,256]{2,1,0:T(8,128)(2,1)S(1)} %get-tuple-element.11), channel_id=1, source_target_pairs={{8,0},{16,8},{24,16},{0,24},{9,1},{17,9},{25,17},{1,25},{10,2},{18... | collective-permute-start | bytes 73736 | tf_op jit(solution)/shard_map/ppermute | solution.py:184
  96.4 1.1 %fusion.1 = (bf16[16,48,1]{2,1,0:T(8,128)(2,1)S(1)}, bf16[16,48,1]{2,1,0:T(8,128)(2,1)S(1)}) fusion(bf16[16,48,256]{2,1,0:T(8,128)(2,1)} %shard_map.67.x_ref), kind=kLoop, calls=%fused_computation.5 | loop fusion | bytes 6144 | tf_op jit(solution)/shard_map/slice | solution.py:186
  98.3 3.5 %collective-permute-start.8 = (bf16[48,16]{1,0:T(8,128)(2,1)S(1)}, bf16[48,16]{1,0:T(8,128)(2,1)S(1)}, u32[]{:S(2)}, u32[]{:S(2)}) collective-permute-start(bf16[48,16]{1,0:T(8,128)(2,1)S(1)} %bitcast.34), channel_id=1, source_target_pairs={{1,0},{2,1},{3,2},{4,3},{5,4},{6,5},{7,6},{0,7},{9,8},{10,9},{11,1... | collective-permute-start | bytes 4616 | tf_op jit(solution)/shard_map/ppermute | solution.py:186
  101.9 1.0 collective-permute-done.7
  105.3 2.3 %shard_map.68 = bf16[16,48,256]{2,1,0:T(8,128)(2,1)} custom-call(bf16[16,48,256]{2,1,0:T(8,128)(2,1)} %shard_map.67.x_ref, bf16[1,48,256]{2,1,0:T(8,128)(2,1)} %copy-done.3, bf16[1,48,256]{2,1,0:T(8,128)(2,1)} %copy-done.5, f32[48,16]{1,0:T(8,128)} %convert_element_type.22.lf_ref, f32[48,16]{1,0:T(8,128)} %convert_element_type.23.rt_ref), custom_call_target="tpu_custom_call" | custom-call | tf_op jit(solution)/shard_map/pallas_call | solution.py:266
  107.6 1.9 %copy.32 = bf16[48,16,256]{2,1,0:T(8,128)(2,1)} copy(bf16[48,16,256]{2,0,1:T(8,128)(2,1)} %bitcast.29) | data formatting | bytes 786432 | tf_op jit(solution)/shard_map/transpose | solution.py:273
  (40 shorter events, 7.8 us)
Async XLA Ops:
  10.2 7.0 %collective-permute-start = (bf16[4,400,256]{2,1,0:T(8,128)(2,1)}, bf16[4,400,256]{2,1,0:T(8,128)(2,1)S(1)}, u32[]{:S(2)}, u32[]{:S(2)}) collective-permute-start(bf16[4,400,256]{2,1,0:T(8,128)(2,1)} %shard_map.65), channel_id=1, source_target_pairs={{0,1},{1,0},{2,3},{3,2},{4,5},{5,4},{6,7},{7,6},{8,9},{9,8},{10,11... | collective-permute-start | bytes 2457608 | tf_op jit(solution)/shard_map/ppermute | solution.py:230
  17.2 8.4 %copy-start.1 = (bf16[48,16,256]{2,1,0:T(8,128)(2,1)S(1)}, bf16[48,16,256]{2,1,0:T(8,128)(2,1)}, u32[]{:S(2)}) copy-start(bf16[48,16,256]{2,1,0:T(8,128)(2,1)} %param.6) | copy-start | bytes 1179652
  19.8 30.1 %all-to-all-start = ((bf16[4,400,256]{2,1,0:T(8,128)(2,1)}), bf16[4,400,256]{2,1,0:T(8,128)(2,1)}, u32[]{:S(2)}, u32[]{:S(2)}) async-start(bf16[4,400,256]{2,1,0:T(8,128)(2,1)} %add_convert_fusion), calls=%async_computation | async-start | bytes 1638400 | tf_op jit(solution)/shard_map/all_to_all | solution.py:234
  28.6 20.1 %collective-permute-start.3 = (bf16[48,16]{1,0:T(8,128)(2,1)S(1)}, bf16[48,16]{1,0:T(8,128)(2,1)S(1)}, u32[]{:S(2)}, u32[]{:S(2)}) collective-permute-start(bf16[48,16]{1,0:T(8,128)(2,1)S(1)} %get-tuple-element.6), channel_id=1, source_target_pairs={{0,1},{1,2},{2,3},{3,4},{4,5},{5,6},{6,7},{7,0},{8,9},{9,10},{10,1... | collective-permute-start | bytes 4616 | tf_op jit(solution)/shard_map/ppermute | solution.py:185
  28.9 20.4 %collective-permute-start.4 = (bf16[48,16]{1,0:T(8,128)(2,1)S(1)}, bf16[48,16]{1,0:T(8,128)(2,1)S(1)}, u32[]{:S(2)}, u32[]{:S(2)}) collective-permute-start(bf16[48,16]{1,0:T(8,128)(2,1)S(1)} %get-tuple-element.5), channel_id=1, source_target_pairs={{1,0},{2,1},{3,2},{4,3},{5,4},{6,5},{7,6},{0,7},{9,8},{10,9},{11,1... | collective-permute-start | bytes 4616 | tf_op jit(solution)/shard_map/ppermute | solution.py:186
  36.2 6.3 %copy-start = (bf16[1,48,256]{0,1,2:T(8,128)(2,1)S(1)}, bf16[1,48,256]{0,1,2:T(8,128)(2,1)}, u32[]{:S(2)}) copy-start(bf16[1,48,256]{0,1,2:T(8,128)(2,1)} %get-tuple-element.7) | copy-start | bytes 73732
  36.2 10.3 %copy-start.6 = (f32[112,48]{0,1:T(8,128)S(1)}, f32[112,48]{0,1:T(8,128)}, u32[]{:S(2)}) copy-start(f32[112,48]{0,1:T(8,128)} %param.9) | copy-start | bytes 64516
  36.2 11.0 %copy-start.7 = (f32[112]{0:T(128)S(1)}, f32[112]{0:T(128)}, u32[]{:S(2)}) copy-start(f32[112]{0:T(128)} %param.10) | copy-start | bytes 1348
  36.2 11.7 %copy-start.8 = (f32[112]{0:T(128)S(1)}, f32[112]{0:T(128)}, u32[]{:S(2)}) copy-start(f32[112]{0:T(128)} %param.11) | copy-start | bytes 1348
  40.9 38.3 %collective-permute-start.1 = (bf16[1,48,256]{2,1,0:T(8,128)(2,1)S(1)}, bf16[1,48,256]{2,1,0:T(8,128)(2,1)S(1)}, u32[]{:S(2)}, u32[]{:S(2)}) collective-permute-start(bf16[1,48,256]{2,1,0:T(8,128)(2,1)S(1)} %copy.27), channel_id=1, source_target_pairs={{0,8},{8,16},{16,24},{24,0},{1,9},{9,17},{17,25},{25,1},{2,10},{10... | collective-permute-start | bytes 73736 | tf_op jit(solution)/shard_map/ppermute | solution.py:183
  45.0 34.2 %collective-permute-start.2 = (bf16[1,48,256]{2,1,0:T(8,128)(2,1)S(1)}, bf16[1,48,256]{2,1,0:T(8,128)(2,1)S(1)}, u32[]{:S(2)}, u32[]{:S(2)}) collective-permute-start(bf16[1,48,256]{2,1,0:T(8,128)(2,1)S(1)} %copy.28), channel_id=1, source_target_pairs={{8,0},{16,8},{24,16},{0,24},{9,1},{17,9},{25,17},{1,25},{10,2},{18... | collective-permute-start | bytes 73736 | tf_op jit(solution)/shard_map/ppermute | solution.py:184
  79.2 0.6 copy-start.2
  79.2 0.6 copy-start.4
  93.5 10.6 %collective-permute-start.5 = (bf16[1,48,256]{2,1,0:T(8,128)(2,1)S(1)}, bf16[1,48,256]{2,1,0:T(8,128)(2,1)S(1)}, u32[]{:S(2)}, u32[]{:S(2)}) collective-permute-start(bf16[1,48,256]{2,1,0:T(8,128)(2,1)S(1)} %get-tuple-element.12), channel_id=1, source_target_pairs={{0,8},{8,16},{16,24},{24,0},{1,9},{9,17},{17,25},{25,1},{2,10},{10... | collective-permute-start | bytes 73736 | tf_op jit(solution)/shard_map/ppermute | solution.py:183
  94.0 10.1 %collective-permute-start.6 = (bf16[1,48,256]{2,1,0:T(8,128)(2,1)S(1)}, bf16[1,48,256]{2,1,0:T(8,128)(2,1)S(1)}, u32[]{:S(2)}, u32[]{:S(2)}) collective-permute-start(bf16[1,48,256]{2,1,0:T(8,128)(2,1)S(1)} %get-tuple-element.11), channel_id=1, source_target_pairs={{8,0},{16,8},{24,16},{0,24},{9,1},{17,9},{25,17},{1,25},{10,2},{18... | collective-permute-start | bytes 73736 | tf_op jit(solution)/shard_map/ppermute | solution.py:184
  97.9 4.9 %collective-permute-start.7 = (bf16[48,16]{1,0:T(8,128)(2,1)S(1)}, bf16[48,16]{1,0:T(8,128)(2,1)S(1)}, u32[]{:S(2)}, u32[]{:S(2)}) collective-permute-start(bf16[48,16]{1,0:T(8,128)(2,1)S(1)} %bitcast.33), channel_id=1, source_target_pairs={{0,1},{1,2},{2,3},{3,4},{4,5},{5,6},{6,7},{7,0},{8,9},{9,10},{10,1... | collective-permute-start | bytes 4616 | tf_op jit(solution)/shard_map/ppermute | solution.py:185
  98.3 5.1 %collective-permute-start.8 = (bf16[48,16]{1,0:T(8,128)(2,1)S(1)}, bf16[48,16]{1,0:T(8,128)(2,1)S(1)}, u32[]{:S(2)}, u32[]{:S(2)}) collective-permute-start(bf16[48,16]{1,0:T(8,128)(2,1)S(1)} %bitcast.34), channel_id=1, source_target_pairs={{1,0},{2,1},{3,2},{4,3},{5,4},{6,5},{7,6},{0,7},{9,8},{10,9},{11,1... | collective-permute-start | bytes 4616 | tf_op jit(solution)/shard_map/ppermute | solution.py:186
  104.1 0.6 copy-start.3
  104.7 0.6 copy-start.5
where the time goes:
time: 110 us; the launch traced here: 109 us
  Pallas kernels  40.7 us (37%)
  local copies, waits for them, and re-layouts  26.5 us (24%)
  starting transfers between devices  19.5 us (18%)
  blocking collectives  16.8 us (15%)
  other arithmetic  4.98 us (5%)
    all_gather x1, blocking collectives, on_device(): tables = lax.all_gather(table, 'tile', axis=0)  16.8 us
    pallas_call x2, Pallas kernels, partial_sums(): pl.pallas_call(functools.partial(partial_kernel, chunks), out_shape=jax.S...  13 us
    pallas_call x1, Pallas kernels, on_device(): pl.pallas_call(functools.partial(gather_kernel, levels), out_shape=jax.Sh...  12.8 us
    pallas_call x1, Pallas kernels, on_device(): pl.pallas_call(functools.partial(radiate_kernel, levels, feats), out_shap...  12.5 us
    unnamed x23, local copies, waits for them, and re-layouts  8.11 us
    slice x3, local copies, waits for them, and re-layouts, halos(): dn = lax.ppermute(x[:1], 'grp', back(g))  7.35 us
    ppermute x2, starting transfers between devices, halos(): rt = lax.ppermute(jnp.transpose(x[:, :, 0]), 'tile', back(t)).astype(F32)  6.87 us
    all_to_all x1, starting transfers between devices, on_device(): lax.all_to_all(partial, 'tile', split_axis=0, concat_axis=0, tiled=True,...  5.86 us
  transfers between devices with their start and end apart: 10, of which 1 were waited for; matrix products, arithmetic and copies ran while one was open for 19% of the time, Pallas kernels for 17%

commit v1 on v0

--- a/solution.py
+++ b/solution.py
@@ -273,9 +273,408 @@
     return jnp.transpose(out, (1, 0, 2))
 
 
+class Layout:
+    def __init__(self, tiles, levels, rows, lanes, gpts):
+        self.tiles, self.levels, self.rows, self.lanes, self.gpts = tiles, levels, rows, lanes, gpts
+        self.bits = tiles.bit_length() - 1
+        self.owned = rows * lanes // 4
+        self.chunks = self.owned // lanes
+        self.feats = 2 * levels
+        self.cells = rows * lanes
+        order = [0]
+        for b in reversed(range(self.bits)):
+            order = order + [s ^ (1 << b) for s in order]
+        self.order = order
+        self.half = tiles // 2
+        self.block = self.half * self.feats + 16
+
+    def message(self, b):
+        return (self.tiles >> (b + 1)) * self.feats + 16
+
+
+def fused_fits(tiles, levels, rows, lanes, gpts):
+    if tiles & (tiles - 1) or tiles < 4 or tiles > 16:
+        return False
+    if levels % 16 or lanes != 256 or rows % 16 or gpts % 8:
+        return False
+    lay = Layout(tiles, levels, rows, lanes, gpts)
+    big = 2 * (2 * lay.block + lay.owned) * lay.cells
+    return big <= VMEM_LIMIT // 2
+
+
+def fused_kernel(lay, *refs):
+    (temp_in, humid_in, parent_ref, kabs_in, planck_in, top_in, out_ref,
+     raw, wide, x, h, onehot, masked, keep, *rest) = refs
+    inb, rest = rest[: lay.bits], rest[lay.bits :]
+    outb, rest = rest[: lay.bits], rest[lay.bits :]
+    (tables, kabs, gvec, trans, net, emit, absorb, heat, sec, edge_out, edge_in, row_in,
+     in_sem, stage_send, stage_recv, tab_send, tab_recv, halo_send, halo_recv) = rest
+    L, R, W, T, C = lay.levels, lay.rows, lay.lanes, lay.tiles, lay.chunks
+    F, G, order = lay.feats, lay.gpts, lay.order
+    octets = G // 8
+    grp, me = lax.axis_index("grp"), lax.axis_index("tile")
+    n_grp = lax.axis_size("grp")
+    south, north = lax.rem(grp + 1, n_grp), lax.rem(grp + n_grp - 1, n_grp)
+    east, west = lax.rem(me + 1, T), lax.rem(me + T - 1, T)
+    MESH = pl.DeviceIdType.MESH
+
+    def peer(d):
+        return me + sum((1 - 2 * lax.rem(me // (1 << b), 2)) * (1 << b) for b in range(lay.bits) if d >> b & 1)
+
+    loads = [
+        pltpu.make_async_copy(temp_in, raw.at[0], in_sem.at[0]),
+        pltpu.make_async_copy(humid_in, raw.at[1], in_sem.at[1]),
+    ]
+    for c in loads:
+        c.start()
+
+    barrier = pltpu.get_barrier_semaphore()
+    friends = [(grp, peer(d)) for d in [1] + list(range(2, T, 2))]
+    friends += [(south, me), (north, me), (grp, east), (grp, west)]
+    for f in friends:
+        pl.semaphore_signal(barrier, inc=1, device_id=f, device_id_type=MESH)
+    pl.semaphore_wait(barrier, len(friends))
+
+    def remote(src, dst, send, recv, to):
+        return pltpu.make_async_remote_copy(
+            src_ref=src, dst_ref=dst, send_sem=send, recv_sem=recv, device_id=to, device_id_type=MESH
+        )
+
+    def stage_copy(b, c):
+        return remote(outb[b].at[c], inb[b].at[c], stage_send.at[b, c], stage_recv.at[b, c], (grp, peer(1 << b)))
+
+    def table_at(s, c):
+        start = c * W if isinstance(c, int) else pl.multiple_of(c * W, W)
+        return tables.at[pl.ds(s * L, L), pl.ds(start, W)]
+
+    def table_copy(d, c):
+        return remote(table_at(0, c), table_at(d, c), tab_send.at[d, c], tab_recv.at[d, c], (grp, peer(d)))
+
+    def forward_copy(d, c):
+        return remote(table_at(d, c), table_at(d ^ 1, c), tab_send.at[d ^ 1, c], tab_recv.at[d ^ 1, c], (grp, peer(1)))
+
+    def halo_copies(field, k):
+        src = [field.at[R - 1], field.at[0], edge_out.at[k, 0], edge_out.at[k, 1]]
+        dst = [row_in.at[k, 0], row_in.at[k, 1], edge_in.at[k, 0], edge_in.at[k, 1]]
+        to = [(south, me), (north, me), (grp, east), (grp, west)]
+        return [remote(src[i], dst[i], halo_send.at[k, i], halo_recv.at[k, i], to[i]) for i in range(4)]
+
+    line = lax.broadcasted_iota(jnp.int32, (W, W), 0)
+
+    def build_onehot(c):
+        for r in range(R):
+            low = parent_ref[r : r + 1, :] % lay.owned - c * W
+            onehot[c * W : (c + 1) * W, r * W : (r + 1) * W] = (line == low).astype(F32).astype(BF16)
+
+    build_onehot(0)
+
+    for i, dst in enumerate((x, h)):
+        loads[i].wait()
+        for k in range(L):
+            level = raw[i, k].astype(F32)
+            for j in range(W // 128):
+                wide[j, k * R : (k + 1) * R, :] = level[:, j * 128 : (j + 1) * 128]
+        for r in range(R):
+            for j in range(W // 128):
+                dst[r, :, j * 128 : (j + 1) * 128] = wide[j, pl.ds(r, L, stride=R), :].astype(BF16)
+
+    def build_masked(half):
+        base = half * lay.block
+        slots = order[half * lay.half : (half + 1) * lay.half]
+        row = lax.broadcasted_iota(jnp.int32, (16, W), 0)
+        want = jnp.full((16, W), -1, jnp.int32)
+        for i, s in enumerate(slots):
+            want = jnp.where(row // 2 == i, peer(s), want)
+        for r in range(R):
+            part = slice(r * W, (r + 1) * W)
+            owner = jnp.broadcast_to(parent_ref[r : r + 1, :] // lay.owned, (16, W))
+            for i, s in enumerate(slots):
+                mask = (owner == peer(s)).astype(F32).astype(BF16)
+                for v in range(L // 16):
+                    src = slice(v * 16, (v + 1) * 16)
+                    at = base + i * F + v * 16
+                    masked[at : at + 16, part] = x[r, src, :] * mask
+                    masked[at + L : at + L + 16, part] = h[r, src, :] * mask
+            at = base + lay.half * F
+            masked[at : at + 16, part] = (owner == want).astype(F32).astype(BF16)
+
+    def partial(c, half):
+        base = half * lay.block
+        total = lax.dot_general(
+            masked[base : base + lay.block, :],
+            onehot[c * W : (c + 1) * W, :],
+            (((1,), (1,)), ((), ())),
+            preferred_element_type=F32,
+        )
+        count = total[lay.half * F :]
+        high = jnp.floor(count * (1.0 / 32.0))
+        row = lax.broadcasted_iota(jnp.int32, (16, W), 0)
+        count = jnp.where(row % 2 == 0, high, count - 32.0 * high)
+        return total[: lay.half * F], count
+
+    def first_stage(c):
+        data, count = partial(c, 1)
+        outb[0][c, : lay.half * F] = data.astype(BF16)
+        outb[0][c, lay.half * F :] = count.astype(BF16)
+        stage_copy(0, c).start()
+        data, count = partial(c, 0)
+        keep[c, : lay.half * F] = data
+        keep[c, lay.half * F :] = count
+
+    def combine(b, c):
+        n = T >> b
+        size, cnt = n * F, lay.half * F
+        stage_copy(b - 1, c).wait_recv()
+        count = keep[c, cnt : cnt + 16] + inb[b - 1][c, size : size + 16].astype(F32)
+        keep[c, cnt : cnt + 16] = count
+        if b == lay.bits:
+            keep[c, :size] = keep[c, :size] + inb[b - 1][c, :size].astype(F32)
+            return
+        cut = size // 2
+        outb[b][c, :cut] = (keep[c, cut:size] + inb[b - 1][c, cut:size].astype(F32)).astype(BF16)
+        outb[b][c, cut : cut + 16] = pltpu.roll(count, 16 - n, 0).astype(BF16)
+        stage_copy(b, c).start()
+        keep[c, :cut] = keep[c, :cut] + inb[b - 1][c, :cut].astype(F32)
+
+    build_masked(1)
+    build_masked(0)
+    first_stage(0)
+
+    lane = lax.broadcasted_iota(jnp.int32, (L, 128), 1)
+
+    def send_halo(field, k):
+        right = jnp.zeros((L, 128), F32)
+        left = jnp.zeros((L, 128), F32)
+        for r in range(R):
+            tail = field[r, :, W - 128 :].astype(F32)
+            lead = field[r, :, :128].astype(F32)
+            right = jnp.where(lane == r, pltpu.roll(tail, (r + 1) % 128, 1), right)
+            left = jnp.where(lane == r, pltpu.roll(lead, r, 1) if r else lead, left)
+        edge_out[k, 0] = right.astype(BF16)
+        edge_out[k, 1] = left.astype(BF16)
+        for cp in halo_copies(field, k):
+            cp.start()
+
+    def laplace(field, k, r):
+        centre = field[r].astype(F32)
+        above = (field[r - 1] if r > 0 else row_in[k, 0]).astype(F32)
+        below = (field[r + 1] if r < R - 1 else row_in[k, 1]).astype(F32)
+        lf = edge_in[k, 0].astype(F32)
+        rt = edge_in[k, 1].astype(F32)
+        lf = pltpu.roll(lf, 128 - r, 1) if r else lf
+        rt = pltpu.roll(rt, 127 - r, 1)
+        wst = pltpu.roll(centre, 1, 1)
+        est = pltpu.roll(centre, W - 1, 1)
+        wst = jnp.concatenate([jnp.where(lane == 0, lf, wst[:, :128]), wst[:, 128:]], 1)
+        est = jnp.concatenate([est[:, : W - 128], jnp.where(lane == 127, rt, est[:, W - 128 :])], 1)
+        return centre, above + below + wst + est - 4.0 * centre
+
+    for c in range(1, C):
+        build_onehot(c)
+        first_stage(c)
+        if c == 1:
+            send_halo(x, 0)
+        combine(1, c - 1)
+        if c > 1:
+            for b in range(2, lay.bits):
+                combine(b, c - 2)
+
+    flipped = jnp.transpose(kabs_in[...])
+    for k in range(L):
+        kabs[k] = jnp.broadcast_to(flipped[:, k : k + 1], (G, 128))
+    sub = lax.broadcasted_iota(jnp.int32, (8, 128), 0)
+    for p in range(octets):
+        for i, ref in enumerate((planck_in, top_in)):
+            vec = jnp.zeros((8, 128), F32)
+            for j in range(8):
+                vec = jnp.where(sub == j, ref[p * 8 + j], vec)
+            gvec[i, p] = vec
+
+    combine(1, C - 1)
+
+    group = octets // 2 if octets % 2 == 0 else octets
+    scale = L / G
+
+    def column(c, j):
+        cols = pl.ds(pl.multiple_of(j * 128, 128), 128)
+        cnt_row = lay.half * F
+        cnt = keep[c, cnt_row : cnt_row + 8, cols]
+        cnt = jnp.maximum(cnt[0:1] * 32.0 + cnt[1:2], 1.0)
+        tc = keep[c, 0:L, cols] / cnt
+        hc = keep[c, L:F, cols] / cnt
+        em = jnp.exp(0.25 * tc)
+        emit[0:L, :] = em
+        absorb[...] = jnp.exp(0.5 * hc) * (-math.log2(math.e))
+        heat[...] = -0.5 * hc
+        for k in range(1, L):
+            emit[L + k : L + k + 1, :] = emit[k - 1 : k, :] - emit[k : k + 1, :]
+        for half in range(octets // group):
+            ps = [half * group + p for p in range(group)]
+            wt = [gvec[0, p] for p in ps]
+            first_em = emit[0:1, :]
+            down = [gvec[1, p] - gvec[0, p] * first_em for p in ps]
+            before = None
+            for i, p in enumerate(ps):
+                before = gvec[1, p] if before is None else before + gvec[1, p]
+            for k in range(L):
+                ab = absorb[k : k + 1, :]
+                acc = None
+                dk = emit[L + k : L + k + 1, :] if k else None
+                for i, p in enumerate(ps):
+                    t = jnp.exp2(kabs[k, p * 8 : p * 8 + 8, :] * ab)
+                    trans[k, i] = t
+                    q = down[i] if k == 0 else down[i] + wt[i] * dk
+                    down[i] = t * q
+                    acc = down[i] if acc is None else acc + down[i]
+                net[k + 1] = acc if half == 0 else net[k + 1] + acc
+            last = emit[L - 1 : L, :]
+            up = [0.3 * down[i] - (0.7 * wt[i]) * last for i in range(group)]
+            for k in range(L - 1, -1, -1):
+                acc = None
+                dk = emit[L + k + 1 : L + k + 2, :] if k < L - 1 else None
+                for i in range(group):
+                    q = up[i] if k == L - 1 else up[i] - wt[i] * dk
+                    up[i] = trans[k, i] * q
+                    acc = up[i] if acc is None else acc + up[i]
+                net[k + 1] = net[k + 1] - acc
+            after = None
+            for i in range(group):
+                u0 = up[i] + wt[i] * first_em
+                after = u0 if after is None else after + u0
+            before = before - after
+            net[0] = before if half == 0 else net[0] + before
+        for k in range(L):
+            row = jnp.sum(net[k] - net[k + 1], axis=0, keepdims=True) * scale
+            heat[k : k + 1, :] = heat[k : k + 1, :] + row
+        at = pl.multiple_of(c * W + j * 128, 128)
+        tables[0:L, pl.ds(at, 128)] = heat[...].astype(BF16)
+
+    evens = list(range(2, T, 2))
+
+    def forward(c):
+        for d in evens:
+            table_copy(d, c).wait_recv()
+            forward_copy(d, c).start()
+
+    def chunk(c, carry):
+        combine(lay.bits, c)
+        lax.fori_loop(0, W // 128, lambda j, s: (column(c, j), s)[1], 0)
+        for d in [1] + evens:
+            table_copy(d, c).start()
+
+        @pl.when(c < C - 2)
+        def _():
+            for b in range(2, lay.bits):
+                combine(b, c + 2)
+
+        @pl.when(c > 0)
+        def _():
+            forward(c - 1)
+
+        return carry
+
+    lax.fori_loop(0, C, chunk, 0)
+
+    forward(C - 1)
+    for cp in halo_copies(x, 0):
+        cp.wait_recv()
+    for c in range(C):
+        for d in [1] + [e ^ 1 for e in evens]:
+            table_copy(d, c).wait_recv()
+
+    for r in range(R):
+        got = jnp.dot(tables[...], onehot[:, r * W : (r + 1) * W], preferred_element_type=F32)
+        owner = jnp.broadcast_to(parent_ref[r : r + 1, :] // lay.owned, (L, W))
+        picked = got[:L]
+        for s in range(1, T):
+            picked = jnp.where(owner == peer(s), got[s * L : (s + 1) * L], picked)
+        centre, lap = laplace(x, 0, r)
+        first = (centre + 0.2 * lap).astype(BF16).astype(F32)
+        heat_f = picked + 0.5 * h[r].astype(F32)
+        sec[r] = (first + 0.5 * heat_f).astype(BF16)
+
+    send_halo(sec, 1)
+    for cp in halo_copies(sec, 1):
+        cp.wait_recv()
+    for r in range(R):
+        centre, lap = laplace(sec, 1, r)
+        out_ref[r] = (centre + 0.2 * lap).astype(BF16)
+
+    for c in range(C):
+        for b in range(lay.bits):
+            stage_copy(b, c).wait_send()
+        for d in [1] + evens:
+            table_copy(d, c).wait_send()
+        for d in evens:
+            forward_copy(d, c).wait_send()
+    for k, field in enumerate((x, sec)):
+        for cp in halo_copies(field, k):
+            cp.wait_send()
+
+
+def fused(temp, humid, parent, kabs, planck, top_flux):
+    levels, rows, lanes = temp.shape
+    tiles = lax.axis_size("tile")
+    gpts = kabs.shape[0]
+    lay = Layout(tiles, levels, rows, lanes, gpts)
+    octets = gpts // 8
+    group = octets // 2 if octets % 2 == 0 else octets
+    any_spec = pl.BlockSpec(memory_space=pl.ANY)
+    smem = pl.BlockSpec(memory_space=pltpu.SMEM)
+    dma = pltpu.SemaphoreType.DMA
+    messages = [pltpu.VMEM((lay.chunks, lay.message(b), lanes), BF16) for b in range(lay.bits)]
+    out = pl.pallas_call(
+        functools.partial(fused_kernel, lay),
+        out_shape=jax.ShapeDtypeStruct((rows, levels, lanes), BF16),
+        in_specs=[any_spec, any_spec, VSPEC, VSPEC, smem, smem],
+        out_specs=VSPEC,
+        scratch_shapes=[
+            pltpu.VMEM((2, levels, rows, lanes), BF16),
+            pltpu.VMEM((lanes // 128, levels * rows, 128), F32),
+            pltpu.VMEM((rows, levels, lanes), BF16),
+            pltpu.VMEM((rows, levels, lanes), BF16),
+            pltpu.VMEM((lay.owned, lay.cells), BF16),
+            pltpu.VMEM((2 * lay.block, lay.cells), BF16),
+            pltpu.VMEM((lay.chunks, lay.block, lanes), F32),
+            *messages,
+            *messages,
+            pltpu.VMEM((tiles * levels, lay.owned), BF16),
+            pltpu.VMEM((levels, gpts, 128), F32),
+            pltpu.VMEM((2, octets, 8, 128), F32),
+            pltpu.VMEM((levels, group, 8, 128), F32),
+            pltpu.VMEM((levels + 1, 8, 128), F32),
+            pltpu.VMEM((2 * levels, 128), F32),
+            pltpu.VMEM((levels, 128), F32),
+            pltpu.VMEM((levels, 128), F32),
+            pltpu.VMEM((rows, levels, lanes), BF16),
+            pltpu.VMEM((2, 2, levels, 128), BF16),
+            pltpu.VMEM((2, 2, levels, 128), BF16),
+            pltpu.VMEM((2, 2, levels, lanes), BF16),
+            dma((2,)),
+            dma((lay.bits, lay.chunks)),
+            dma((lay.bits, lay.chunks)),
+            dma((tiles, lay.chunks)),
+            dma((tiles, lay.chunks)),
+            dma((2, 4)),
+            dma((2, 4)),
+        ],
+        compiler_params=pltpu.CompilerParams(
+            collective_id=0, has_side_effects=True, vmem_limit_bytes=VMEM_LIMIT
+        ),
+    )(temp, humid, parent, jnp.transpose(kabs), planck, top_flux)
+    return jnp.transpose(out, (1, 0, 2))
+
+
+def program(*args):
+    tiles = lax.axis_size("tile")
+    if fused_fits(tiles, *args[0].shape, args[3].shape[0]):
+        return fused(*args)
+    return on_device(*args)
+
+
 def solution(mesh):
     return jax.shard_map(
-        on_device,
+        program,
         mesh=mesh,
         in_specs=(P(None, "grp", "tile"), P(None, "grp", "tile"), P("grp", "tile"), P(), P(), P()),
         out_specs=P(None, "grp", "tile"),

time: 110 us -> 56 us (0.51)
  local copies, waits for them, and re-layouts: 26.5 us -> 1.86 us
  starting transfers between devices: 19.5 us -> 0 us
  blocking collectives: 16.8 us -> 0 us
  Pallas kernels: 40.7 us -> 53.9 us
  other arithmetic: 4.98 us -> 0 us
    all_gather x1 -> x0, blocking collectives: 16.8 us -> none  [on_device(): tables = lax.all_gather(table, 'tile', axis=0)]
    ppermute x9 -> x0, starting transfers between devices: 13.6 us -> none  [the longest x2 6.87 us: halos(): rt = lax.ppermute(jnp.transpose(x[:, :, 0]), 'tile', back(t)).astype(F32)]
    pallas_call x5 -> x1, Pallas kernels: 40.7 us -> 53.9 us  [fused(): pl.pallas_call(functools.partial(fused_kernel, lay), out_shape=jax.ShapeD...]
    slice x5 -> x0, local copies, waits for them, and re-layouts: 13.2 us -> none  [the longest x3 7.35 us: halos(): dn = lax.ppermute(x[:1], 'grp', back(g))]
    unnamed x23 -> x0, local copies, waits for them, and re-layouts: 8.11 us -> none
    all_to_all x1 -> x0, starting transfers between devices: 5.86 us -> none  [on_device(): lax.all_to_all(partial, 'tile', split_axis=0, concat_axis=0, tiled=True,...]
    convert_element_type x5 -> x0, other arithmetic: 4.98 us -> none  [the longest x1 2.57 us: on_device(): partial = (mine + given.astype(F32)).astype(BF16)]
    transpose x3 -> x1, local copies, waits for them, and re-layouts: 3.72 us -> 1.86 us  [fused(): return jnp.transpose(out, (1, 0, 2))]
  transfers between devices with their start and end apart: 10 -> 0, of which waited for: 1 -> 0; matrix products, arithmetic and copies ran while one was open for 19% -> 0% of each run, Pallas kernels for 17% -> 0%
where the time goes in v1:
time: 56 us; the launch traced here: 55.8 us
  Pallas kernels  53.9 us (96%)
  local copies, waits for them, and re-layouts  1.86 us (3%)
    pallas_call x1, Pallas kernels, fused(): pl.pallas_call(functools.partial(fused_kernel, lay), out_shape=jax.ShapeD...  53.9 us
    transpose x1, local copies, waits for them, and re-layouts, fused(): return jnp.transpose(out, (1, 0, 2))  1.86 us

profile of v1, /device:TPU:0, one launch (start us, length us, event | category | flops | bytes accessed | tf_op | source)
XLA Modules:
  0.0 55.8 jit_solution(16971423560702962724)
XLA Ops:
  0.0 53.9 %shard_map.64 = bf16[16,48,256]{2,1,0:T(8,128)(2,1)} custom-call(bf16[48,16,256]{2,1,0:T(8,128)(2,1)} %refs_0_.1, bf16[48,16,256]{2,1,0:T(8,128)(2,1)} %refs_1_.1, s32[16,256]{1,0:T(8,128)} %refs_2_.1, f32[48,112]{1,0:T(8,128)} %bitcast.3, f32[112]{0:T(128)} %refs_4_.1, f32[112]{0:T(128)} %refs_5_.1), custom_call_target="tpu_custom_call" | custom-call | tf_op jit(solution)/shard_map/pallas_call | solution.py:626
  53.9 1.9 %copy.7 = bf16[48,16,256]{2,1,0:T(8,128)(2,1)} copy(bf16[48,16,256]{2,0,1:T(8,128)(2,1)} %bitcast.2) | data formatting | bytes 786432 | tf_op jit(solution)/shard_map/transpose | solution.py:665

commit v2 on v1

--- a/solution.py
+++ b/solution.py
@@ -280,37 +280,42 @@
         self.owned = rows * lanes // 4
         self.chunks = self.owned // lanes
         self.feats = 2 * levels
+        self.per = lanes // 128
+        self.pieces = self.chunks * self.per
         self.cells = rows * lanes
         order = [0]
         for b in reversed(range(self.bits)):
             order = order + [s ^ (1 << b) for s in order]
         self.order = order
-        self.half = tiles // 2
-        self.block = self.half * self.feats + 16
+        self.quarter = tiles // 4
+        self.block = self.quarter * self.feats + 16
 
     def message(self, b):
-        return (self.tiles >> (b + 1)) * self.feats + 16
+        return self.block if b < 2 else (self.tiles >> (b + 1)) * self.feats + 16
 
 
 def fused_fits(tiles, levels, rows, lanes, gpts):
-    if tiles & (tiles - 1) or tiles < 4 or tiles > 16:
+    if tiles & (tiles - 1) or tiles < 4 or tiles > 16 or rows < 16:
         return False
     if levels % 16 or lanes != 256 or rows % 16 or gpts % 8:
         return False
     lay = Layout(tiles, levels, rows, lanes, gpts)
-    big = 2 * (2 * lay.block + lay.owned) * lay.cells
-    return big <= VMEM_LIMIT // 2
+    big = 2 * (4 * lay.block + lay.owned) * lay.cells
+    return lay.chunks >= 4 and big <= VMEM_LIMIT // 2
 
 
 def fused_kernel(lay, *refs):
     (temp_in, humid_in, parent_ref, kabs_in, planck_in, top_in, out_ref,
-     raw, wide, x, h, onehot, masked, keep, *rest) = refs
-    inb, rest = rest[: lay.bits], rest[lay.bits :]
-    outb, rest = rest[: lay.bits], rest[lay.bits :]
-    (tables, kabs, gvec, trans, net, emit, absorb, heat, sec, edge_out, edge_in, row_in,
-     in_sem, stage_send, stage_recv, tab_send, tab_recv, halo_send, halo_recv) = rest
+     raw, wide, x, h, onehot, masked, keep, pair_in, pair_out, *rest) = refs
+    inb, rest = rest[: lay.bits - 1], rest[lay.bits - 1 :]
+    outb, rest = rest[: lay.bits - 1], rest[lay.bits - 1 :]
+    (tables, kabs, gvec, trans, net, emit, absorb, heat, base, sec, edge_out, edge_in, row_in,
+     rim_out, rim_in, rimp_out, rimp_in, rimhot,
+     in_sem, pair_send, pair_recv, stage_send, stage_recv, tab_send, tab_recv,
+     halo_send, halo_recv, rim_send, rim_recv) = rest
     L, R, W, T, C = lay.levels, lay.rows, lay.lanes, lay.tiles, lay.chunks
-    F, G, order = lay.feats, lay.gpts, lay.order
+    N, per = lay.pieces, lay.per
+    F, G, Q, B, order = lay.feats, lay.gpts, lay.quarter, lay.block, lay.order
     octets = G // 8
     grp, me = lax.axis_index("grp"), lax.axis_index("tile")
     n_grp = lax.axis_size("grp")
@@ -333,19 +338,23 @@
     friends += [(south, me), (north, me), (grp, east), (grp, west)]
     for f in friends:
         pl.semaphore_signal(barrier, inc=1, device_id=f, device_id_type=MESH)
-    pl.semaphore_wait(barrier, len(friends))
 
     def remote(src, dst, send, recv, to):
         return pltpu.make_async_remote_copy(
             src_ref=src, dst_ref=dst, send_sem=send, recv_sem=recv, device_id=to, device_id_type=MESH
         )
 
+    def pair_copy(i, c):
+        return remote(pair_out.at[i, c], pair_in.at[i, c], pair_send.at[i, c], pair_recv.at[i, c], (grp, peer(1)))
+
     def stage_copy(b, c):
-        return remote(outb[b].at[c], inb[b].at[c], stage_send.at[b, c], stage_recv.at[b, c], (grp, peer(1 << b)))
+        return remote(
+            outb[b - 1].at[c], inb[b - 1].at[c], stage_send.at[b, c], stage_recv.at[b, c], (grp, peer(1 << b))
+        )
 
     def table_at(s, c):
-        start = c * W if isinstance(c, int) else pl.multiple_of(c * W, W)
-        return tables.at[pl.ds(s * L, L), pl.ds(start, W)]
+        start = c * 128 if isinstance(c, int) else pl.multiple_of(c * 128, 128)
+        return tables.at[pl.ds(s * L, L), pl.ds(start, 128)]
 
     def table_copy(d, c):
         return remote(table_at(0, c), table_at(d, c), tab_send.at[d, c], tab_recv.at[d, c], (grp, peer(d)))
@@ -353,11 +362,24 @@
     def forward_copy(d, c):
         return remote(table_at(d, c), table_at(d ^ 1, c), tab_send.at[d ^ 1, c], tab_recv.at[d ^ 1, c], (grp, peer(1)))
 
-    def halo_copies(field, k):
-        src = [field.at[R - 1], field.at[0], edge_out.at[k, 0], edge_out.at[k, 1]]
-        dst = [row_in.at[k, 0], row_in.at[k, 1], edge_in.at[k, 0], edge_in.at[k, 1]]
-        to = [(south, me), (north, me), (grp, east), (grp, west)]
-        return [remote(src[i], dst[i], halo_send.at[k, i], halo_recv.at[k, i], to[i]) for i in range(4)]
+    def row_copies(field, k):
+        return [
+            remote(field.at[R - 1], row_in.at[k, 0], halo_send.at[k, 0], halo_recv.at[k, 0], (south, me)),
+            remote(field.at[0], row_in.at[k, 1], halo_send.at[k, 1], halo_recv.at[k, 1], (north, me)),
+        ]
+
+    def edge_copies():
+        return [
+            remote(edge_out.at[i], edge_in.at[i], halo_send.at[2, i], halo_recv.at[2, i], (grp, to))
+            for i, to in enumerate((east, west))
+        ]
+
+    def rim_copies():
+        return [
+            remote(src.at[i], dst.at[i], rim_send.at[n, i], rim_recv.at[n, i], (grp, to))
+            for n, (src, dst) in enumerate(((rim_out, rim_in), (rimp_out, rimp_in)))
+            for i, to in enumerate((east, west))
+        ]
 
     line = lax.broadcasted_iota(jnp.int32, (W, W), 0)
 
@@ -378,9 +400,13 @@
             for j in range(W // 128):
                 dst[r, :, j * 128 : (j + 1) * 128] = wide[j, pl.ds(r, L, stride=R), :].astype(BF16)
 
-    def build_masked(half):
-        base = half * lay.block
-        slots = order[half * lay.half : (half + 1) * lay.half]
+    def slots_of(quarter):
+        at = {0: 3, 1: 2, 2: 1, 3: 0}[quarter] * Q
+        return order[at : at + Q]
+
+    def build_masked(quarter):
+        start = quarter * B
+        slots = slots_of(quarter)
         row = lax.broadcasted_iota(jnp.int32, (16, W), 0)
         want = jnp.full((16, W), -1, jnp.int32)
         for i, s in enumerate(slots):
@@ -392,57 +418,73 @@
                 mask = (owner == peer(s)).astype(F32).astype(BF16)
                 for v in range(L // 16):
                     src = slice(v * 16, (v + 1) * 16)
-                    at = base + i * F + v * 16
+                    at = start + i * F + v * 16
                     masked[at : at + 16, part] = x[r, src, :] * mask
                     masked[at + L : at + L + 16, part] = h[r, src, :] * mask
-            at = base + lay.half * F
+            at = start + Q * F
             masked[at : at + 16, part] = (owner == want).astype(F32).astype(BF16)
 
-    def partial(c, half):
-        base = half * lay.block
-        total = lax.dot_general(
-            masked[base : base + lay.block, :],
-            onehot[c * W : (c + 1) * W, :],
-            (((1,), (1,)), ((), ())),
-            preferred_element_type=F32,
-        )
-        count = total[lay.half * F :]
-        high = jnp.floor(count * (1.0 / 32.0))
+    def partial(c, first, n):
+        dots = []
+        for base_q in (first, first + 2):
+            total = lax.dot_general(
+                masked[base_q * B : (base_q + n) * B, :],
+                onehot[c * W : (c + 1) * W, :],
+                (((1,), (1,)), ((), ())),
+                preferred_element_type=F32,
+            )
+            dots.append(total)
         row = lax.broadcasted_iota(jnp.int32, (16, W), 0)
-        count = jnp.where(row % 2 == 0, high, count - 32.0 * high)
-        return total[: lay.half * F], count
-
-    def first_stage(c):
-        data, count = partial(c, 1)
-        outb[0][c, : lay.half * F] = data.astype(BF16)
-        outb[0][c, lay.half * F :] = count.astype(BF16)
-        stage_copy(0, c).start()
-        data, count = partial(c, 0)
-        keep[c, : lay.half * F] = data
-        keep[c, lay.half * F :] = count
+        for half, total in enumerate(dots):
+            for i in range(n):
+                data = total[i * B : i * B + Q * F]
+                count = total[i * B + Q * F : (i + 1) * B]
+                high = jnp.floor(count * (1.0 / 32.0))
+                count = jnp.where(row % 2 == 0, high, count - 32.0 * high)
+                ref, dtype = ((pair_out, BF16), (keep, F32))[half]
+                for j in range(per):
+                    cols = slice(j * 128, (j + 1) * 128)
+                    ref[first + i, c * per + j, : Q * F] = data[:, cols].astype(dtype)
+                    ref[first + i, c * per + j, Q * F :] = count[:, cols].astype(dtype)
+        for i in range(n):
+            for j in range(per):
+                pair_copy(first + i, c * per + j).start()
 
     def combine(b, c):
+        if b == 1:
+            pair_copy(0, c).wait_recv()
+            outb[0][c] = (keep[0, c] + pair_in[0, c].astype(F32)).astype(BF16)
+            stage_copy(1, c).start()
+            return
         n = T >> b
-        size, cnt = n * F, lay.half * F
-        stage_copy(b - 1, c).wait_recv()
-        count = keep[c, cnt : cnt + 16] + inb[b - 1][c, size : size + 16].astype(F32)
-        keep[c, cnt : cnt + 16] = count
+        size, cnt = n * F, Q * F
+        if b == 2:
+            pair_copy(1, c).wait_recv()
+            stage_copy(1, c).wait_recv()
+            got = lambda part: pair_in[1, c, part].astype(F32) + inb[0][c, part].astype(F32)
+            count = keep[1, c, cnt : cnt + 16] + got(slice(cnt, cnt + 16))
+        else:
+            stage_copy(b - 1, c).wait_recv()
+            got = lambda part: inb[b - 2][c, part].astype(F32)
+            count = keep[1, c, cnt : cnt + 16] + got(slice(size, size + 16))
+        keep[1, c, cnt : cnt + 16] = count
         if b == lay.bits:
-            keep[c, :size] = keep[c, :size] + inb[b - 1][c, :size].astype(F32)
+            keep[1, c, :size] = keep[1, c, :size] + got(slice(0, size))
             return
         cut = size // 2
-        outb[b][c, :cut] = (keep[c, cut:size] + inb[b - 1][c, cut:size].astype(F32)).astype(BF16)
-        outb[b][c, cut : cut + 16] = pltpu.roll(count, 16 - n, 0).astype(BF16)
+        outb[b - 1][c, :cut] = (keep[1, c, cut:size] + got(slice(cut, size))).astype(BF16)
+        outb[b - 1][c, cut : cut + 16] = pltpu.roll(count, 16 - n, 0).astype(BF16)
         stage_copy(b, c).start()
-        keep[c, :cut] = keep[c, :cut] + inb[b - 1][c, :cut].astype(F32)
-
-    build_masked(1)
-    build_masked(0)
-    first_stage(0)
+        keep[1, c, :cut] = keep[1, c, :cut] + got(slice(0, cut))
+
+    def middle(c):
+        for b in range(2, lay.bits):
+            combine(b, c)
 
     lane = lax.broadcasted_iota(jnp.int32, (L, 128), 1)
-
-    def send_halo(field, k):
+    spot = lax.broadcasted_iota(jnp.int32, (8, 128), 1)
+
+    def columns(field):
         right = jnp.zeros((L, 128), F32)
         left = jnp.zeros((L, 128), F32)
         for r in range(R):
@@ -450,34 +492,43 @@
             lead = field[r, :, :128].astype(F32)
             right = jnp.where(lane == r, pltpu.roll(tail, (r + 1) % 128, 1), right)
             left = jnp.where(lane == r, pltpu.roll(lead, r, 1) if r else lead, left)
-        edge_out[k, 0] = right.astype(BF16)
-        edge_out[k, 1] = left.astype(BF16)
-        for cp in halo_copies(field, k):
-            cp.start()
-
-    def laplace(field, k, r):
+        return right, left
+
+    def laplace(field, k, r, lf, rt):
         centre = field[r].astype(F32)
         above = (field[r - 1] if r > 0 else row_in[k, 0]).astype(F32)
         below = (field[r + 1] if r < R - 1 else row_in[k, 1]).astype(F32)
-        lf = edge_in[k, 0].astype(F32)
-        rt = edge_in[k, 1].astype(F32)
-        lf = pltpu.roll(lf, 128 - r, 1) if r else lf
-        rt = pltpu.roll(rt, 127 - r, 1)
         wst = pltpu.roll(centre, 1, 1)
         est = pltpu.roll(centre, W - 1, 1)
         wst = jnp.concatenate([jnp.where(lane == 0, lf, wst[:, :128]), wst[:, 128:]], 1)
         est = jnp.concatenate([est[:, : W - 128], jnp.where(lane == 127, rt, est[:, W - 128 :])], 1)
-        return centre, above + below + wst + est - 4.0 * centre
-
+        return (centre + 0.2 * (above + below + wst + est - 4.0 * centre)).astype(BF16)
+
+    build_masked(0)
+    build_masked(2)
+    pl.semaphore_wait(barrier, len(friends))
+    partial(0, 0, 1)
+    build_masked(1)
+    build_masked(3)
+    build_onehot(1)
+    partial(0, 1, 1)
+    for i in range(per):
+        combine(1, i)
+    sent = per
     for c in range(1, C):
-        build_onehot(c)
-        first_stage(c)
+        if c + 1 < C:
+            build_onehot(c + 1)
+        partial(c, 0, 2)
         if c == 1:
-            send_halo(x, 0)
-        combine(1, c - 1)
+            for i, edge in enumerate(columns(x)):
+                edge_out[i] = edge.astype(BF16)
+            for cp in row_copies(x, 0) + edge_copies():
+                cp.start()
+        if c == C - 1:
+            middle(0)
         if c > 1:
-            for b in range(2, lay.bits):
-                combine(b, c - 2)
+            combine(1, sent)
+            sent += 1
 
     flipped = jnp.transpose(kabs_in[...])
     for k in range(L):
@@ -490,20 +541,45 @@
                 vec = jnp.where(sub == j, ref[p * 8 + j], vec)
             gvec[i, p] = vec
 
-    combine(1, C - 1)
+    for cp in row_copies(x, 0) + edge_copies():
+        cp.wait_recv()
+    for r in range(R):
+        lf = edge_in[0].astype(F32)
+        lf = pltpu.roll(lf, 128 - r, 1) if r else lf
+        rt = pltpu.roll(edge_in[1].astype(F32), 127 - r, 1)
+        base[r] = laplace(x, 0, r, lf, rt).astype(F32) + 0.25 * h[r].astype(F32)
+    for i, edge in enumerate(columns(base)):
+        rim_out[i] = edge
+    right = jnp.full((8, 128), -1, jnp.int32)
+    left = jnp.full((8, 128), -1, jnp.int32)
+    for r in range(R):
+        line_r = jnp.broadcast_to(parent_ref[r : r + 1, :], (8, W))
+        right = jnp.where(spot == r, pltpu.roll(line_r[:, W - 128 :], (r + 1) % 128, 1), right)
+        left = jnp.where(spot == r, pltpu.roll(line_r[:, :128], r, 1) if r else line_r[:, :128], left)
+    rimp_out[0] = right
+    rimp_out[1] = left
+    for cp in rim_copies():
+        cp.start()
+    lead = N // 2
+    for i in range(1, lead):
+        if i == lead - 1:
+            for k in range(sent, N - 1):
+                combine(1, k)
+            sent = N - 1
+        middle(i)
+        if sent < N:
+            combine(1, sent)
+            sent += 1
 
     group = octets // 2 if octets % 2 == 0 else octets
     scale = L / G
 
-    def column(c, j):
-        cols = pl.ds(pl.multiple_of(j * 128, 128), 128)
-        cnt_row = lay.half * F
-        cnt = keep[c, cnt_row : cnt_row + 8, cols]
+    def column(c):
+        cnt = keep[1, c, Q * F : Q * F + 8]
         cnt = jnp.maximum(cnt[0:1] * 32.0 + cnt[1:2], 1.0)
-        tc = keep[c, 0:L, cols] / cnt
-        hc = keep[c, L:F, cols] / cnt
-        em = jnp.exp(0.25 * tc)
-        emit[0:L, :] = em
+        tc = keep[1, c, 0:L] / cnt
+        hc = keep[1, c, L:F] / cnt
+        emit[0:L, :] = jnp.exp(0.25 * tc)
         absorb[...] = jnp.exp(0.5 * hc) * (-math.log2(math.e))
         heat[...] = -0.5 * hc
         for k in range(1, L):
@@ -514,7 +590,7 @@
             first_em = emit[0:1, :]
             down = [gvec[1, p] - gvec[0, p] * first_em for p in ps]
             before = None
-            for i, p in enumerate(ps):
+            for p in ps:
                 before = gvec[1, p] if before is None else before + gvec[1, p]
             for k in range(L):
                 ab = absorb[k : k + 1, :]
@@ -546,7 +622,7 @@
         for k in range(L):
             row = jnp.sum(net[k] - net[k + 1], axis=0, keepdims=True) * scale
             heat[k : k + 1, :] = heat[k : k + 1, :] + row
-        at = pl.multiple_of(c * W + j * 128, 128)
+        at = pl.multiple_of(c * 128, 128)
         tables[0:L, pl.ds(at, 128)] = heat[...].astype(BF16)
 
     evens = list(range(2, T, 2))
@@ -556,60 +632,85 @@
             table_copy(d, c).wait_recv()
             forward_copy(d, c).start()
 
-    def chunk(c, carry):
-        combine(lay.bits, c)
-        lax.fori_loop(0, W // 128, lambda j, s: (column(c, j), s)[1], 0)
+    def piece(i, carry):
+        combine(lay.bits, i)
+        column(i)
         for d in [1] + evens:
-            table_copy(d, c).start()
-
-        @pl.when(c < C - 2)
+            table_copy(d, i).start()
+
+        @pl.when(i < N - lead)
         def _():
-            for b in range(2, lay.bits):
-                combine(b, c + 2)
-
-        @pl.when(c > 0)
+            middle(i + lead)
+
+        @pl.when(i >= lag)
         def _():
-            forward(c - 1)
+            forward(i - lag)
 
         return carry
 
-    lax.fori_loop(0, C, chunk, 0)
-
-    forward(C - 1)
-    for cp in halo_copies(x, 0):
-        cp.wait_recv()
-    for c in range(C):
-        for d in [1] + [e ^ 1 for e in evens]:
-            table_copy(d, c).wait_recv()
-
-    for r in range(R):
-        got = jnp.dot(tables[...], onehot[:, r * W : (r + 1) * W], preferred_element_type=F32)
-        owner = jnp.broadcast_to(parent_ref[r : r + 1, :] // lay.owned, (L, W))
+    lag = N // 2
+    lax.fori_loop(0, N, piece, 0)
+
+    arrivals = [1] + [e ^ 1 for e in evens]
+
+    def pick(hot, span, owner):
+        got = jnp.dot(tables[:, span], hot, preferred_element_type=F32)
         picked = got[:L]
         for s in range(1, T):
             picked = jnp.where(owner == peer(s), got[s * L : (s + 1) * L], picked)
-        centre, lap = laplace(x, 0, r)
-        first = (centre + 0.2 * lap).astype(BF16).astype(F32)
-        heat_f = picked + 0.5 * h[r].astype(F32)
-        sec[r] = (first + 0.5 * heat_f).astype(BF16)
-
-    send_halo(sec, 1)
-    for cp in halo_copies(sec, 1):
+        return picked
+
+    def gather(r, span):
+        owner = jnp.broadcast_to(parent_ref[r : r + 1, :] // lay.owned, (L, W))
+        return base[r] + 0.5 * pick(onehot[span, r * W : (r + 1) * W], span, owner)
+
+    early, late = slice(0, (N - lag) * 128), slice((N - lag) * 128, N * 128)
+    for i in range(N - lag):
+        for d in arrivals:
+            table_copy(d, i).wait_recv()
+    for r in range(R):
+        base[r] = gather(r, early)
+        if r % (R // lag) == R // lag - 1:
+            forward(N - lag + r // (R // lag))
+
+    for cp in rim_copies():
+        cp.wait_recv()
+    rimp = jnp.where(spot < R, rimp_in[0], jnp.where(spot < 2 * R, pltpu.roll(rimp_in[1], R, 1), -1))
+    low = rimp[0:1, :] % lay.owned
+    tall = lax.broadcasted_iota(jnp.int32, (W, 128), 0)
+    for c in range(C):
+        rimhot[c * W : (c + 1) * W, :] = (tall == low - c * W).astype(F32).astype(BF16)
+
+    for i in range(N - lag, N):
+        for d in arrivals:
+            table_copy(d, i).wait_recv()
+    for r in [0, R - 1] + list(range(1, R - 1)):
+        sec[r] = gather(r, late).astype(BF16)
+        if r == R - 1:
+            for cp in row_copies(sec, 1):
+                cp.start()
+    owner = jnp.broadcast_to(rimp[0:1, :] // lay.owned, (L, 128))
+    rim = jnp.where(lane < R, rim_in[0], pltpu.roll(rim_in[1], R, 1))
+    rim = (rim + 0.5 * pick(rimhot[...], slice(0, C * W), owner)).astype(BF16).astype(F32)
+
+    for cp in row_copies(sec, 1):
         cp.wait_recv()
     for r in range(R):
-        centre, lap = laplace(sec, 1, r)
-        out_ref[r] = (centre + 0.2 * lap).astype(BF16)
-
-    for c in range(C):
-        for b in range(lay.bits):
+        lf = pltpu.roll(rim, 128 - r, 1) if r else rim
+        rt = pltpu.roll(rim, 127 - R - r, 1)
+        out_ref[r] = laplace(sec, 1, r, lf, rt)
+
+    for c in range(N):
+        for i in range(2):
+            pair_copy(i, c).wait_send()
+        for b in range(1, lay.bits):
             stage_copy(b, c).wait_send()
         for d in [1] + evens:
             table_copy(d, c).wait_send()
         for d in evens:
             forward_copy(d, c).wait_send()
-    for k, field in enumerate((x, sec)):
-        for cp in halo_copies(field, k):
-            cp.wait_send()
+    for cp in row_copies(x, 0) + edge_copies() + rim_copies() + row_copies(sec, 1):
+        cp.wait_send()
 
 
 def fused(temp, humid, parent, kabs, planck, top_flux):
@@ -622,7 +723,7 @@
     any_spec = pl.BlockSpec(memory_space=pl.ANY)
     smem = pl.BlockSpec(memory_space=pltpu.SMEM)
     dma = pltpu.SemaphoreType.DMA
-    messages = [pltpu.VMEM((lay.chunks, lay.message(b), lanes), BF16) for b in range(lay.bits)]
+    messages = [pltpu.VMEM((lay.pieces, lay.message(b), 128), BF16) for b in range(1, lay.bits)]
     out = pl.pallas_call(
         functools.partial(fused_kernel, lay),
         out_shape=jax.ShapeDtypeStruct((rows, levels, lanes), BF16),
@@ -634,8 +735,10 @@
             pltpu.VMEM((rows, levels, lanes), BF16),
             pltpu.VMEM((rows, levels, lanes), BF16),
             pltpu.VMEM((lay.owned, lay.cells), BF16),
-            pltpu.VMEM((2 * lay.block, lay.cells), BF16),
-            pltpu.VMEM((lay.chunks, lay.block, lanes), F32),
+            pltpu.VMEM((4 * lay.block, lay.cells), BF16),
+            pltpu.VMEM((2, lay.pieces, lay.block, 128), F32),
+            pltpu.VMEM((2, lay.pieces, lay.block, 128), BF16),
+            pltpu.VMEM((2, lay.pieces, lay.block, 128), BF16),
             *messages,
             *messages,
             pltpu.VMEM((tiles * levels, lay.owned), BF16),
@@ -646,17 +749,27 @@
             pltpu.VMEM((2 * levels, 128), F32),
             pltpu.VMEM((levels, 128), F32),
             pltpu.VMEM((levels, 128), F32),
+            pltpu.VMEM((rows, levels, lanes), F32),
             pltpu.VMEM((rows, levels, lanes), BF16),
-            pltpu.VMEM((2, 2, levels, 128), BF16),
-            pltpu.VMEM((2, 2, levels, 128), BF16),
+            pltpu.VMEM((2, levels, 128), BF16),
+            pltpu.VMEM((2, levels, 128), BF16),
             pltpu.VMEM((2, 2, levels, lanes), BF16),
+            pltpu.VMEM((2, levels, 128), F32),
+            pltpu.VMEM((2, levels, 128), F32),
+            pltpu.VMEM((2, 8, 128), jnp.int32),
+            pltpu.VMEM((2, 8, 128), jnp.int32),
+            pltpu.VMEM((lay.owned, 128), BF16),
             dma((2,)),
-            dma((lay.bits, lay.chunks)),
-            dma((lay.bits, lay.chunks)),
-            dma((tiles, lay.chunks)),
-            dma((tiles, lay.chunks)),
-            dma((2, 4)),
-            dma((2, 4)),
+            dma((2, lay.pieces)),
+            dma((2, lay.pieces)),
+            dma((lay.bits, lay.pieces)),
+            dma((lay.bits, lay.pieces)),
+            dma((tiles, lay.pieces)),
+            dma((tiles, lay.pieces)),
+            dma((3, 2)),
+            dma((3, 2)),
+            dma((2, 2)),
+            dma((2, 2)),
         ],
         compiler_params=pltpu.CompilerParams(
             collective_id=0, has_side_effects=True, vmem_limit_bytes=VMEM_LIMIT

time: 56 us -> 53.1 us (0.948)
  Pallas kernels: 53.9 us -> 51 us
    pallas_call x1, Pallas kernels: 53.9 us -> 51 us  [fused(): pl.pallas_call(functools.partial(fused_kernel, lay), out_shape=jax.ShapeD...]
where the time goes in v2:
time: 53.1 us; the launch traced here: 52.9 us
  Pallas kernels  51 us (96%)
  local copies, waits for them, and re-layouts  1.86 us (4%)
    pallas_call x1, Pallas kernels, fused(): pl.pallas_call(functools.partial(fused_kernel, lay), out_shape=jax.ShapeD...  51 us
    transpose x1, local copies, waits for them, and re-layouts, fused(): return jnp.transpose(out, (1, 0, 2))  1.86 us

profile of v2, /device:TPU:0, one launch (start us, length us, event | category | flops | bytes accessed | tf_op | source)
XLA Modules:
  0.0 52.9 jit_solution(6308618910121060132)
XLA Ops:
  0.0 51.0 %shard_map.64 = bf16[16,48,256]{2,1,0:T(8,128)(2,1)} custom-call(bf16[48,16,256]{2,1,0:T(8,128)(2,1)} %refs_0_.1, bf16[48,16,256]{2,1,0:T(8,128)(2,1)} %refs_1_.1, s32[16,256]{1,0:T(8,128)} %refs_2_.1, f32[48,112]{1,0:T(8,128)} %bitcast.3, f32[112]{0:T(128)} %refs_4_.1, f32[112]{0:T(128)} %refs_5_.1), custom_call_target="tpu_custom_call" | custom-call | tf_op jit(solution)/shard_map/pallas_call | solution.py:727
  51.0 1.9 %copy.7 = bf16[48,16,256]{2,1,0:T(8,128)(2,1)} copy(bf16[48,16,256]{2,0,1:T(8,128)(2,1)} %bitcast.2) | data formatting | bytes 786432 | tf_op jit(solution)/shard_map/transpose | solution.py:778

commit v3 on v2

--- a/solution.py
+++ b/solution.py
@@ -384,9 +384,13 @@
     line = lax.broadcasted_iota(jnp.int32, (W, W), 0)
 
     def build_onehot(c):
-        for r in range(R):
-            low = parent_ref[r : r + 1, :] % lay.owned - c * W
-            onehot[c * W : (c + 1) * W, r * W : (r + 1) * W] = (line == low).astype(F32).astype(BF16)
+        def row(r, carry):
+            low = parent_ref[pl.ds(r, 1), :] % lay.owned - c * W
+            at = pl.ds(pl.multiple_of(r * W, W), W)
+            onehot[c * W : (c + 1) * W, at] = (line == low).astype(F32).astype(BF16)
+            return carry
+
+        lax.fori_loop(0, R, row, 0)
 
     build_onehot(0)
 
@@ -514,7 +518,6 @@
     partial(0, 1, 1)
     for i in range(per):
         combine(1, i)
-    sent = per
     for c in range(1, C):
         if c + 1 < C:
             build_onehot(c + 1)
@@ -524,11 +527,10 @@
                 edge_out[i] = edge.astype(BF16)
             for cp in row_copies(x, 0) + edge_copies():
                 cp.start()
-        if c == C - 1:
-            middle(0)
         if c > 1:
-            combine(1, sent)
-            sent += 1
+            for i in range((c - 1) * per, c * per):
+                combine(1, i)
+            middle(c - 2)
 
     flipped = jnp.transpose(kabs_in[...])
     for k in range(L):
@@ -540,6 +542,9 @@
             for j in range(8):
                 vec = jnp.where(sub == j, ref[p * 8 + j], vec)
             gvec[i, p] = vec
+    for i in range(N - per, N):
+        combine(1, i)
+    middle(C - 2)
 
     for cp in row_copies(x, 0) + edge_copies():
         cp.wait_recv()
@@ -561,15 +566,8 @@
     for cp in rim_copies():
         cp.start()
     lead = N // 2
-    for i in range(1, lead):
-        if i == lead - 1:
-            for k in range(sent, N - 1):
-                combine(1, k)
-            sent = N - 1
+    for i in range(C - 1, lead):
         middle(i)
-        if sent < N:
-            combine(1, sent)
-            sent += 1
 
     group = octets // 2 if octets % 2 == 0 else octets
     scale = L / G
@@ -634,13 +632,14 @@
 
     def piece(i, carry):
         combine(lay.bits, i)
+
+        @pl.when(i < N - lead)
+        def _():
+            middle(i + lead)
+
         column(i)
         for d in [1] + evens:
             table_copy(d, i).start()
-
-        @pl.when(i < N - lead)
-        def _():
-            middle(i + lead)
 
         @pl.when(i >= lag)
         def _():

time: 53.1 us -> 52.2 us (0.983)
  Pallas kernels: 51 us -> 50.1 us
    pallas_call x1, Pallas kernels: 51 us -> 50.1 us  [fused(): pl.pallas_call(functools.partial(fused_kernel, lay), out_shape=jax.ShapeD...]
where the time goes in v3:
time: 52.2 us; the launch traced here: 52 us
  Pallas kernels  50.1 us (96%)
  local copies, waits for them, and re-layouts  1.86 us (4%)
    pallas_call x1, Pallas kernels, fused(): pl.pallas_call(functools.partial(fused_kernel, lay), out_shape=jax.ShapeD...  50.1 us
    transpose x1, local copies, waits for them, and re-layouts, fused(): return jnp.transpose(out, (1, 0, 2))  1.86 us

profile of v3, /device:TPU:0, one launch (start us, length us, event | category | flops | bytes accessed | tf_op | source)
XLA Modules:
  0.0 52.0 jit_solution(1563710750155092387)
XLA Ops:
  0.0 50.1 %shard_map.64 = bf16[16,48,256]{2,1,0:T(8,128)(2,1)} custom-call(bf16[48,16,256]{2,1,0:T(8,128)(2,1)} %refs_0_.1, bf16[48,16,256]{2,1,0:T(8,128)(2,1)} %refs_1_.1, s32[16,256]{1,0:T(8,128)} %refs_2_.1, f32[48,112]{1,0:T(8,128)} %bitcast.3, f32[112]{0:T(128)} %refs_4_.1, f32[112]{0:T(128)} %refs_5_.1), custom_call_target="tpu_custom_call" | custom-call | tf_op jit(solution)/shard_map/pallas_call | solution.py:726
  50.1 1.9 %copy.7 = bf16[48,16,256]{2,1,0:T(8,128)(2,1)} copy(bf16[48,16,256]{2,0,1:T(8,128)(2,1)} %bitcast.2) | data formatting | bytes 786432 | tf_op jit(solution)/shard_map/transpose | solution.py:777
